TPU v7x, 32 devices: a whole 2x2x4 slice. The times are simulated.
32 devices in a mesh: src: 8 (over y, x, core), dst: 4 (over z).
Axes of the slice: x: 2, y: 2, z: 4, core: 2. Of those that a mesh axis runs over, the one named last changes fastest.
Arguments:
- raw: bfloat16 [4096, 256], P(('src', 'dst')), may hold values from -6 to 6
- enc_w1: bfloat16 [256, 512], replicated, may hold values from -0.375 to 0.375
- enc_w2: bfloat16 [512, 256], replicated, may hold values from -0.25 to 0.25
- block_weights: float32 [512, 128, 128], P(('src', 'dst')), may hold values from -0.125 to 0.125
- block_cols: int32 [512], P(('src', 'dst')), may hold values from 0 to 3, as said below
- noise: bfloat16 [3, 4096, 256], P(None, ('src', 'dst')), may hold values from -3 to 3
Outputs:
- encoded: bfloat16 [4096, 256], P(('src', 'dst'))
- hops: bfloat16 [3, 4096, 256], P(None, ('src', 'dst'))
Inputs may be any that keep to these rules, and one draw needn't show every extreme that they name: `block_cols`: entry b of each device's 16 entries belongs to row block b // 2; row blocks 2j and 2j+1 of a device together name every column block exactly once, each naming 4 // 2 distinct ones.
All inputs are finite; a program needn't handle non-finite values.
Results may differ from a plain program's by a relative error of at most 0.0058.
Values may be sent and summed in bfloat16 or wider, within the bound.
A program may use at most 128 MiB of HBM per device.

v0:
```python
import jax
import jax.numpy as jnp
from jax import lax
from jax.sharding import PartitionSpec as P

HOPS = 3


def normalize_rows(z):
    return (z * lax.rsqrt(jnp.mean(z * z, axis=-1, keepdims=True) + 1e-06)).astype(jnp.bfloat16)


def shards(raw, enc_w1, enc_w2, block_weights, block_cols, noise):
    hidden = jax.nn.silu(jnp.dot(raw, enc_w1, preferred_element_type=jnp.float32)).astype(
        jnp.bfloat16
    )
    encoded = normalize_rows(jnp.dot(hidden, enc_w2, preferred_element_type=jnp.float32))
    own_rows = raw.shape[0]
    block_side = block_weights.shape[1]
    width = encoded.shape[1]
    feats = encoded
    kept = []
    for step in range(HOPS):
        group = lax.all_gather(feats, "dst", axis=0, tiled=True)
        col_count = group.shape[0] // block_side
        half = col_count // 2
        col_blocks = group.astype(jnp.float32).reshape(col_count, block_side, width)
        fetched = jnp.take(col_blocks, block_cols, axis=0)
        prods = jnp.einsum("bij,bjw->biw", block_weights, fetched, precision=lax.Precision.HIGHEST)
        mine = lax.psum_scatter(
            prods.reshape(own_rows * lax.axis_size("src") // block_side, half, block_side, width)
            .sum(axis=1)
            .reshape(own_rows * lax.axis_size("src"), width),
            "src",
            scatter_dimension=0,
            tiled=True,
        )
        feats = normalize_rows(mine + noise[step].astype(jnp.float32))
        kept.append(feats)
    return (encoded, jnp.stack(kept))


def solution(mesh):
    placed = (
        P(("src", "dst"), None),
        P(),
        P(),
        P(("src", "dst"), None, None),
        P(("src", "dst")),
        P(None, ("src", "dst"), None),
    )
    return jax.shard_map(
        shards,
        mesh=mesh,
        in_specs=placed,
        out_specs=(P(("src", "dst"), None), P(None, ("src", "dst"), None)),
        check_vma=False,
    )
```

profile of v0, /device:TPU:0, one launch (start us, length us, event | category | flops | bytes accessed | tf_op | source)
XLA Modules:
  0.0 204.7 jit_solution(9608763618662152512)
XLA Ops:
  7.2 0.0 reduce-scatter.4.cloned.1.call-start
  7.2 0.7 compare_and_fusion
  8.0 0.7 compare_select_fusion
  8.6 1.5 multiply_reduce_fusion.3
  10.1 0.1 multiply_convert_fusion.4
  10.2 15.7 %all_gather.9 = bf16[512,256]{1,0:T(8,128)(2,1)S(1)} all-gather(bf16[128,256]{1,0:T(8,128)(2,1)S(1)} %multiply_convert_fusion.4), channel_id=1, replica_groups=mesh['src'=8,'dst'=4] {'dst'}, dimensions={0}, use_global_device_ids=true | all-gather | bytes 327680 | tf_op jit(solution)/shard_map/all_gather | solution.py:24
  25.9 2.0 gather_fusion
  28.0 5.4 %bitcast_reduce_fusion.2 = f32[8,128,256]{1,2,0:T(8,128)S(1)} fusion(f32[16,128,128]{2,1,0:T(8,128)S(1)} %copy-done, f32[16,128,256]{2,1,0:T(8,128)} %gather_fusion, pred[16]{0:T(512)(128)(4,1)S(1)} %compare_and_fusion), kind=kOutput, calls=%fused_computation.5 | convolution fusion | flops 806092800 | bytes 4194320 | tf_op jit(solution)/shard_map/bij,bjw->biw/dot_general | solution.py:29
  33.4 1.3 copy.15
  34.8 0.0 reduce-scatter.4.cloned.1.call-update
  34.8 0.0 reduce-scatter.6.cloned.1.call-start
  34.9 37.6 %reduce-scatter.4.cloned.1.call-done = f32[128,256]{1,0:T(8,128)} async-done(((f32[1024,256]{1,0:T(8,128)}), f32[128,256]{1,0:T(8,128)}) %reduce-scatter.4.cloned.1.call-update) | async-done | bytes 131088 | tf_op jit(solution)/shard_map/reduce_scatter | solution.py:30
  72.4 1.0 multiply_reduce_fusion.2
  73.5 1.0 multiply_convert_fusion.3
  74.5 13.8 %all_gather.10 = bf16[512,256]{1,0:T(8,128)(2,1)S(1)} all-gather(bf16[128,256]{1,0:T(8,128)(2,1)S(1)} %multiply_convert_fusion.3), channel_id=1, replica_groups=mesh['src'=8,'dst'=4] {'dst'}, dimensions={0}, use_global_device_ids=true | all-gather | bytes 327680 | tf_op jit(solution)/shard_map/all_gather | solution.py:24
  88.3 2.0 gather_fusion.1
  90.4 5.4 %bitcast_reduce_fusion.1 = f32[8,128,256]{1,2,0:T(8,128)S(1)} fusion(f32[16,128,128]{2,1,0:T(8,128)S(1)} %copy-done, f32[16,128,256]{2,1,0:T(8,128)} %gather_fusion.1, pred[16]{0:T(512)(128)(4,1)S(1)} %compare_and_fusion), kind=kOutput, calls=%fused_computation.4 | convolution fusion | flops 806092800 | bytes 4194320 | tf_op jit(solution)/shard_map/bij,bjw->biw/dot_general | solution.py:29
  95.8 1.3 copy.17
  97.2 0.0 reduce-scatter.6.cloned.1.call-update
  97.2 0.0 reduce-scatter.8.cloned.1.call-start
  97.2 36.7 %reduce-scatter.6.cloned.1.call-done = f32[128,256]{1,0:T(8,128)} async-done(((f32[1024,256]{1,0:T(8,128)}), f32[128,256]{1,0:T(8,128)}) %reduce-scatter.6.cloned.1.call-update) | async-done | bytes 131088 | tf_op jit(solution)/shard_map/reduce_scatter | solution.py:30
  133.9 1.0 multiply_reduce_fusion.1
  134.9 1.0 multiply_convert_fusion.2
  135.9 14.1 %all_gather.11 = bf16[512,256]{1,0:T(8,128)(2,1)S(1)} all-gather(bf16[128,256]{1,0:T(8,128)(2,1)S(1)} %multiply_convert_fusion.2), channel_id=1, replica_groups=mesh['src'=8,'dst'=4] {'dst'}, dimensions={0}, use_global_device_ids=true | all-gather | bytes 327680 | tf_op jit(solution)/shard_map/all_gather | solution.py:24
  150.0 2.0 gather_fusion.2
  152.1 5.4 %bitcast_reduce_fusion = f32[8,128,256]{1,2,0:T(8,128)S(1)} fusion(f32[16,128,128]{2,1,0:T(8,128)S(1)} %copy-done, f32[16,128,256]{2,1,0:T(8,128)} %gather_fusion.2, pred[16]{0:T(512)(128)(4,1)S(1)} %compare_and_fusion), kind=kOutput, calls=%fused_computation.3 | convolution fusion | flops 806092800 | bytes 4194320 | tf_op jit(solution)/shard_map/bij,bjw->biw/dot_general | solution.py:29
  157.5 1.3 copy.19
  158.8 0.0 reduce-scatter.8.cloned.1.call-update
  158.9 36.6 %reduce-scatter.8.cloned.1.call-done = f32[128,256]{1,0:T(8,128)} async-done(((f32[1024,256]{1,0:T(8,128)}), f32[128,256]{1,0:T(8,128)}) %reduce-scatter.8.cloned.1.call-update) | async-done | bytes 131088 | tf_op jit(solution)/shard_map/reduce_scatter | solution.py:30
  195.5 1.0 multiply_reduce_fusion
  196.5 1.0 fusion.19
  197.5 0.7 pad_maximum_fusion
  (14 shorter events, 0.2 us)
Async XLA Ops:
  7.2 20.8 %copy-start = (f32[16,128,128]{2,1,0:T(8,128)S(1)}, f32[16,128,128]{2,1,0:T(8,128)}, u32[]{:S(2)}) copy-start(f32[16,128,128]{2,1,0:T(8,128)} %param.11) | copy-start | bytes 3145732
  7.2 65.3 %reduce-scatter.4.cloned.1.call-start = ((), (), s32[]{:S(2)}) async-start(), calls=%async_computation.3 | async-start | bytes 1179648 | tf_op jit(solution)/shard_map/reduce_scatter | solution.py:30
  10.2 17.7 %copy-start.2 = (bf16[128,256]{1,0:T(8,128)(2,1)}, bf16[128,256]{1,0:T(8,128)(2,1)S(1)}, u32[]{:S(2)}) copy-start(bf16[128,256]{1,0:T(8,128)(2,1)S(1)} %multiply_convert_fusion.4) | copy-start | bytes 196612
  33.4 39.0 %copy-start.1 = (bf16[3,128,256]{2,1,0:T(8,128)(2,1)S(1)}, bf16[3,128,256]{2,1,0:T(8,128)(2,1)}, u32[]{:S(2)}) copy-start(bf16[3,128,256]{2,1,0:T(8,128)(2,1)} %param.13) | copy-start | bytes 589828
  34.8 99.1 %reduce-scatter.6.cloned.1.call-start = ((), (), s32[]{:S(2)}) async-start(), calls=%async_computation.4 | async-start | bytes 1179648 | tf_op jit(solution)/shard_map/reduce_scatter | solution.py:30
  97.2 98.3 %reduce-scatter.8.cloned.1.call-start = ((), (), s32[]{:S(2)}) async-start(), calls=%async_computation.5 | async-start | bytes 1179648 | tf_op jit(solution)/shard_map/reduce_scatter | solution.py:30
Sparse Core Ops, SparseCore 0:
  34.9 37.4 reduce-scatter.3
  97.3 36.5 reduce-scatter.5
  159.0 36.4 reduce-scatter.7
where the time goes:
time: 205 us
  waiting for transfers between devices  111 us (54%)
  blocking collectives  43.6 us (21%)
  matrix products  17.8 us (9%)
  between operations  13.9 us (7%)
  local copies, waits for them, and re-layouts  10.1 us (5%)
  other arithmetic  8.34 us (4%)
    reduce_scatter x3, waiting for transfers between devices, shards(): lax.psum_scatter(prods.reshape(own_rows * lax.axis_size('src') // block_s...  111 us
    all_gather x3, blocking collectives, shards(): group = lax.all_gather(feats, 'dst', axis=0, tiled=True)  43.6 us
    dot_general x3, matrix products, shards(): jnp.einsum('bij,bjw->biw', block_weights, fetched, precision=lax.Precisio...  16.3 us
    gather x3, local copies, waits for them, and re-layouts, shards(): fetched = jnp.take(col_blocks, block_cols, axis=0)  6.1 us
  transfers between devices with their start and end apart: 3, of which 3 were waited for; matrix products, arithmetic and copies ran while one was open for 0% of the time, Pallas kernels for 0%

commit v1 on v0

--- a/solution.py
+++ b/solution.py
@@ -21,7 +21,14 @@
     feats = encoded
     kept = []
     for step in range(HOPS):
-        group = lax.all_gather(feats, "dst", axis=0, tiled=True)
+        ways, here = (lax.axis_size("dst"), lax.axis_index("dst"))
+        group, reach = (feats, 1)
+        while reach < ways:
+            theirs = lax.ppermute(group, "dst", [(d, d ^ reach) for d in range(ways)])
+            mine_first = jnp.concatenate([group, theirs], axis=0)
+            theirs_first = jnp.concatenate([theirs, group], axis=0)
+            group = jnp.where(here & reach == 0, mine_first, theirs_first)
+            reach = 2 * reach
         col_count = group.shape[0] // block_side
         half = col_count // 2
         col_blocks = group.astype(jnp.float32).reshape(col_count, block_side, width)

time: 205 us -> 196 us (0.956)
  blocking collectives: 43.6 us -> 0 us
  waiting for transfers between devices: 111 us -> 132 us
  starting transfers between devices: 0.12 us -> 14.5 us
    all_gather x3 -> x0, blocking collectives: 43.6 us -> none  [shards(): group = lax.all_gather(feats, 'dst', axis=0, tiled=True)]
    ppermute x0 -> x6, waiting for transfers between devices: none -> 22.3 us  [shards(): theirs = lax.ppermute(group, 'dst', [(d, d ^ reach) for d in range(ways)])]
    ppermute x0 -> x6, starting transfers between devices: none -> 14.2 us  [shards(): theirs = lax.ppermute(group, 'dst', [(d, d ^ reach) for d in range(ways)])]
  transfers between devices with their start and end apart: 3 -> 9, of which waited for: 3 -> 9; matrix products, arithmetic and copies ran while one was open for 0% -> 0% of each run, Pallas kernels for 0% -> 0%
where the time goes in v1:
time: 196 us
  waiting for transfers between devices  132 us (67%)
  matrix products  17.9 us (9%)
  starting transfers between devices  14.5 us (7%)
  between operations  13.9 us (7%)
  local copies, waits for them, and re-layouts  10.1 us (5%)
  other arithmetic  8.01 us (4%)
    reduce_scatter x3, waiting for transfers between devices, shards(): lax.psum_scatter(prods.reshape(own_rows * lax.axis_size('src') // block_s...  109 us
    ppermute x6, waiting for transfers between devices, shards(): theirs = lax.ppermute(group, 'dst', [(d, d ^ reach) for d in range(ways)])  22.3 us
    dot_general x3, matrix products, shards(): jnp.einsum('bij,bjw->biw', block_weights, fetched, precision=lax.Precisio...  16.3 us
    ppermute x6, starting transfers between devices, shards(): theirs = lax.ppermute(group, 'dst', [(d, d ^ reach) for d in range(ways)])  14.2 us
    gather x3, local copies, waits for them, and re-layouts, shards(): fetched = jnp.take(col_blocks, block_cols, axis=0)  6.1 us
    reduce_sum x3, local copies, waits for them, and re-layouts, shards(): mine = lax.psum_scatter(prods.reshape(own_rows * lax.axis_size('src') //...  3.98 us
  transfers between devices with their start and end apart: 9, of which 9 were waited for; matrix products, arithmetic and copies ran while one was open for 0% of the time, Pallas kernels for 0%

profile of v1, /device:TPU:0, one launch (start us, length us, event | category | flops | bytes accessed | tf_op | source)
XLA Modules:
  0.0 196.0 jit_solution(16013972075701003553)
XLA Ops:
  7.2 1.6 multiply_reduce_fusion.3
  8.9 3.1 %collective-permute-start = (bf16[128,256]{1,0:T(8,128)(2,1)S(1)}, bf16[128,256]{1,0:T(8,128)(2,1)S(1)}, u32[]{:S(2)}, u32[]{:S(2)}) collective-permute-start(bf16[128,256]{1,0:T(8,128)(2,1)S(1)} %multiply_convert_fusion.4), channel_id=1, source_target_pairs={{0,1},{1,0},{2,3},{3,2},{4,5},{5,4},{6,7},{7,6},{8,9},{9,8},{10,11... | collective-permute-start | bytes 196616 | tf_op jit(solution)/shard_map/ppermute | solution.py:27
  12.7 1.6 collective-permute-done
  14.3 3.1 %collective-permute-start.1 = (bf16[256,256]{1,0:T(8,128)(2,1)S(1)}, bf16[256,256]{1,0:T(8,128)(2,1)S(1)}, u32[]{:S(2)}, u32[]{:S(2)}) collective-permute-start(bf16[256,256]{1,0:T(8,128)(2,1)S(1)} %maximum_select_fusion.3), channel_id=1, source_target_pairs={{0,2},{1,3},{2,0},{3,1},{4,6},{5,7},{6,4},{7,5},{8,10},{9,11},{10,... | collective-permute-start | bytes 393224 | tf_op jit(solution)/shard_map/ppermute | solution.py:27
  17.4 5.1 %collective-permute-done.1 = bf16[256,256]{1,0:T(8,128)(2,1)S(1)} collective-permute-done((bf16[256,256]{1,0:T(8,128)(2,1)S(1)}, bf16[256,256]{1,0:T(8,128)(2,1)S(1)}, u32[]{:S(2)}, u32[]{:S(2)}) %collective-permute-start.1) | collective-permute-done | bytes 131104 | tf_op jit(solution)/shard_map/ppermute | solution.py:27
  22.7 2.0 %gather_fusion = f32[16,128,256]{2,1,0:T(8,128)} fusion(f32[4,128,256]{2,1,0:T(8,128)S(1)} %convert.6, s32[1024]{0:T(1024)S(1)} %pad_clamp_fusion), kind=kCustom, calls=%fused_computation.clone | custom fusion | bytes 4194368 | tf_op jit(solution)/shard_map/jit(_take)/gather | solution.py:35
  24.8 5.4 %bitcast_reduce_fusion.2 = f32[8,128,256]{1,2,0:T(8,128)S(1)} fusion(f32[16,128,128]{2,1,0:T(8,128)S(1)} %copy-done, f32[16,128,256]{2,1,0:T(8,128)} %gather_fusion, pred[16]{0:T(512)(128)(4,1)S(1)} %compare_and_fusion), kind=kOutput, calls=%fused_computation.5 | convolution fusion | flops 806092800 | bytes 4194320 | tf_op jit(solution)/shard_map/bij,bjw->biw/dot_general | solution.py:36
  30.2 1.3 copy.12
  31.6 37.2 %reduce-scatter.4.cloned.1.call-done = f32[128,256]{1,0:T(8,128)} async-done(((f32[1024,256]{1,0:T(8,128)}), f32[128,256]{1,0:T(8,128)}) %reduce-scatter.4.cloned.1.call-update) | async-done | bytes 131088 | tf_op jit(solution)/shard_map/reduce_scatter | solution.py:37
  68.9 1.0 multiply_reduce_fusion.2
  69.9 1.0 multiply_convert_fusion.3
  70.9 1.6 collective-permute-start.2
  72.5 2.8 %collective-permute-done.2 = bf16[128,256]{1,0:T(8,128)(2,1)S(1)} collective-permute-done((bf16[128,256]{1,0:T(8,128)(2,1)S(1)}, bf16[128,256]{1,0:T(8,128)(2,1)S(1)}, u32[]{:S(2)}, u32[]{:S(2)}) %collective-permute-start.2) | collective-permute-done | bytes 65568 | tf_op jit(solution)/shard_map/ppermute | solution.py:27
  75.2 2.5 %collective-permute-start.3 = (bf16[256,256]{1,0:T(8,128)(2,1)S(1)}, bf16[256,256]{1,0:T(8,128)(2,1)S(1)}, u32[]{:S(2)}, u32[]{:S(2)}) collective-permute-start(bf16[256,256]{1,0:T(8,128)(2,1)S(1)} %maximum_select_fusion.4), channel_id=1, source_target_pairs={{0,2},{1,3},{2,0},{3,1},{4,6},{5,7},{6,4},{7,5},{8,10},{9,11},{10,... | collective-permute-start | bytes 393224 | tf_op jit(solution)/shard_map/ppermute | solution.py:27
  77.7 5.0 %collective-permute-done.3 = bf16[256,256]{1,0:T(8,128)(2,1)S(1)} collective-permute-done((bf16[256,256]{1,0:T(8,128)(2,1)S(1)}, bf16[256,256]{1,0:T(8,128)(2,1)S(1)}, u32[]{:S(2)}, u32[]{:S(2)}) %collective-permute-start.3) | collective-permute-done | bytes 131104 | tf_op jit(solution)/shard_map/ppermute | solution.py:27
  82.9 2.0 %gather_fusion.1 = f32[16,128,256]{2,1,0:T(8,128)} fusion(f32[4,128,256]{2,1,0:T(8,128)S(1)} %convert.8, s32[1024]{0:T(1024)S(1)} %pad_clamp_fusion), kind=kCustom, calls=%fused_computation.1.clone | custom fusion | bytes 4194368 | tf_op jit(solution)/shard_map/jit(_take)/gather | solution.py:35
  84.9 5.4 %bitcast_reduce_fusion.1 = f32[8,128,256]{1,2,0:T(8,128)S(1)} fusion(f32[16,128,128]{2,1,0:T(8,128)S(1)} %copy-done, f32[16,128,256]{2,1,0:T(8,128)} %gather_fusion.1, pred[16]{0:T(512)(128)(4,1)S(1)} %compare_and_fusion), kind=kOutput, calls=%fused_computation.4 | convolution fusion | flops 806092800 | bytes 4194320 | tf_op jit(solution)/shard_map/bij,bjw->biw/dot_general | solution.py:36
  90.4 1.3 copy.14
  92.0 35.9 %reduce-scatter.6.cloned.1.call-done = f32[128,256]{1,0:T(8,128)} async-done(((f32[1024,256]{1,0:T(8,128)}), f32[128,256]{1,0:T(8,128)}) %reduce-scatter.6.cloned.1.call-update) | async-done | bytes 131088 | tf_op jit(solution)/shard_map/reduce_scatter | solution.py:37
  127.8 1.0 multiply_reduce_fusion.1
  128.8 1.0 multiply_convert_fusion.2
  129.9 1.5 collective-permute-start.4
  131.4 2.8 %collective-permute-done.4 = bf16[128,256]{1,0:T(8,128)(2,1)S(1)} collective-permute-done((bf16[128,256]{1,0:T(8,128)(2,1)S(1)}, bf16[128,256]{1,0:T(8,128)(2,1)S(1)}, u32[]{:S(2)}, u32[]{:S(2)}) %collective-permute-start.4) | collective-permute-done | bytes 65568 | tf_op jit(solution)/shard_map/ppermute | solution.py:27
  134.2 2.5 %collective-permute-start.5 = (bf16[256,256]{1,0:T(8,128)(2,1)S(1)}, bf16[256,256]{1,0:T(8,128)(2,1)S(1)}, u32[]{:S(2)}, u32[]{:S(2)}) collective-permute-start(bf16[256,256]{1,0:T(8,128)(2,1)S(1)} %maximum_select_fusion.5), channel_id=1, source_target_pairs={{0,2},{1,3},{2,0},{3,1},{4,6},{5,7},{6,4},{7,5},{8,10},{9,11},{10,... | collective-permute-start | bytes 393224 | tf_op jit(solution)/shard_map/ppermute | solution.py:27
  136.7 5.0 %collective-permute-done.5 = bf16[256,256]{1,0:T(8,128)(2,1)S(1)} collective-permute-done((bf16[256,256]{1,0:T(8,128)(2,1)S(1)}, bf16[256,256]{1,0:T(8,128)(2,1)S(1)}, u32[]{:S(2)}, u32[]{:S(2)}) %collective-permute-start.5) | collective-permute-done | bytes 131104 | tf_op jit(solution)/shard_map/ppermute | solution.py:27
  141.9 2.0 %gather_fusion.2 = f32[16,128,256]{2,1,0:T(8,128)} fusion(f32[4,128,256]{2,1,0:T(8,128)S(1)} %convert.10, s32[1024]{0:T(1024)S(1)} %pad_clamp_fusion), kind=kCustom, calls=%fused_computation.2.clone | custom fusion | bytes 4194368 | tf_op jit(solution)/shard_map/jit(_take)/gather | solution.py:35
  143.9 5.4 %bitcast_reduce_fusion = f32[8,128,256]{1,2,0:T(8,128)S(1)} fusion(f32[16,128,128]{2,1,0:T(8,128)S(1)} %copy-done, f32[16,128,256]{2,1,0:T(8,128)} %gather_fusion.2, pred[16]{0:T(512)(128)(4,1)S(1)} %compare_and_fusion), kind=kOutput, calls=%fused_computation.3 | convolution fusion | flops 806092800 | bytes 4194320 | tf_op jit(solution)/shard_map/bij,bjw->biw/dot_general | solution.py:36
  149.3 1.3 copy.16
  150.7 36.1 %reduce-scatter.8.cloned.1.call-done = f32[128,256]{1,0:T(8,128)} async-done(((f32[1024,256]{1,0:T(8,128)}), f32[128,256]{1,0:T(8,128)}) %reduce-scatter.8.cloned.1.call-update) | async-done | bytes 131088 | tf_op jit(solution)/shard_map/reduce_scatter | solution.py:37
  186.8 1.0 multiply_reduce_fusion
  187.8 1.0 fusion.19
  188.8 0.7 pad_maximum_fusion
  (31 shorter events, 1.7 us)
Async XLA Ops:
  7.2 17.6 %copy-start = (f32[16,128,128]{2,1,0:T(8,128)S(1)}, f32[16,128,128]{2,1,0:T(8,128)}, u32[]{:S(2)}) copy-start(f32[16,128,128]{2,1,0:T(8,128)} %param.11) | copy-start | bytes 3145732
  7.2 10.2 %copy-start.3 = (s32[16]{0:T(128)S(1)}, s32[16]{0:T(128)}, u32[]{:S(2)}) copy-start(s32[16]{0:T(128)} %param.12) | copy-start | bytes 196
  7.2 61.7 %reduce-scatter.4.cloned.1.call-start = ((), (), s32[]{:S(2)}) async-start(), calls=%async_computation.3 | async-start | bytes 1179648 | tf_op jit(solution)/shard_map/reduce_scatter | solution.py:37
  8.9 15.9 %copy-start.2 = (bf16[128,256]{1,0:T(8,128)(2,1)}, bf16[128,256]{1,0:T(8,128)(2,1)S(1)}, u32[]{:S(2)}) copy-start(bf16[128,256]{1,0:T(8,128)(2,1)S(1)} %multiply_convert_fusion.4) | copy-start | bytes 196612
  8.9 5.4 %collective-permute-start = (bf16[128,256]{1,0:T(8,128)(2,1)S(1)}, bf16[128,256]{1,0:T(8,128)(2,1)S(1)}, u32[]{:S(2)}, u32[]{:S(2)}) collective-permute-start(bf16[128,256]{1,0:T(8,128)(2,1)S(1)} %multiply_convert_fusion.4), channel_id=1, source_target_pairs={{0,1},{1,0},{2,3},{3,2},{4,5},{5,4},{6,7},{7,6},{8,9},{9,8},{10,11... | collective-permute-start | bytes 196616 | tf_op jit(solution)/shard_map/ppermute | solution.py:27
  14.3 8.3 %collective-permute-start.1 = (bf16[256,256]{1,0:T(8,128)(2,1)S(1)}, bf16[256,256]{1,0:T(8,128)(2,1)S(1)}, u32[]{:S(2)}, u32[]{:S(2)}) collective-permute-start(bf16[256,256]{1,0:T(8,128)(2,1)S(1)} %maximum_select_fusion.3), channel_id=1, source_target_pairs={{0,2},{1,3},{2,0},{3,1},{4,6},{5,7},{6,4},{7,5},{8,10},{9,11},{10,... | collective-permute-start | bytes 393224 | tf_op jit(solution)/shard_map/ppermute | solution.py:27
  30.2 38.6 %copy-start.1 = (bf16[3,128,256]{2,1,0:T(8,128)(2,1)S(1)}, bf16[3,128,256]{2,1,0:T(8,128)(2,1)}, u32[]{:S(2)}) copy-start(bf16[3,128,256]{2,1,0:T(8,128)(2,1)} %param.13) | copy-start | bytes 589828
  31.6 96.2 %reduce-scatter.6.cloned.1.call-start = ((), (), s32[]{:S(2)}) async-start(), calls=%async_computation.4 | async-start | bytes 1179648 | tf_op jit(solution)/shard_map/reduce_scatter | solution.py:37
  70.9 4.3 %collective-permute-start.2 = (bf16[128,256]{1,0:T(8,128)(2,1)S(1)}, bf16[128,256]{1,0:T(8,128)(2,1)S(1)}, u32[]{:S(2)}, u32[]{:S(2)}) collective-permute-start(bf16[128,256]{1,0:T(8,128)(2,1)S(1)} %multiply_convert_fusion.3), channel_id=1, source_target_pairs={{0,1},{1,0},{2,3},{3,2},{4,5},{5,4},{6,7},{7,6},{8,9},{9,8},{10,11... | collective-permute-start | bytes 196616 | tf_op jit(solution)/shard_map/ppermute | solution.py:27
  75.2 7.5 %collective-permute-start.3 = (bf16[256,256]{1,0:T(8,128)(2,1)S(1)}, bf16[256,256]{1,0:T(8,128)(2,1)S(1)}, u32[]{:S(2)}, u32[]{:S(2)}) collective-permute-start(bf16[256,256]{1,0:T(8,128)(2,1)S(1)} %maximum_select_fusion.4), channel_id=1, source_target_pairs={{0,2},{1,3},{2,0},{3,1},{4,6},{5,7},{6,4},{7,5},{8,10},{9,11},{10,... | collective-permute-start | bytes 393224 | tf_op jit(solution)/shard_map/ppermute | solution.py:27
  91.7 95.0 %reduce-scatter.8.cloned.1.call-start = ((), (), s32[]{:S(2)}) async-start(), calls=%async_computation.5 | async-start | bytes 1179648 | tf_op jit(solution)/shard_map/reduce_scatter | solution.py:37
  129.9 4.3 %collective-permute-start.4 = (bf16[128,256]{1,0:T(8,128)(2,1)S(1)}, bf16[128,256]{1,0:T(8,128)(2,1)S(1)}, u32[]{:S(2)}, u32[]{:S(2)}) collective-permute-start(bf16[128,256]{1,0:T(8,128)(2,1)S(1)} %multiply_convert_fusion.2), channel_id=1, source_target_pairs={{0,1},{1,0},{2,3},{3,2},{4,5},{5,4},{6,7},{7,6},{8,9},{9,8},{10,11... | collective-permute-start | bytes 196616 | tf_op jit(solution)/shard_map/ppermute | solution.py:27
  134.2 7.5 %collective-permute-start.5 = (bf16[256,256]{1,0:T(8,128)(2,1)S(1)}, bf16[256,256]{1,0:T(8,128)(2,1)S(1)}, u32[]{:S(2)}, u32[]{:S(2)}) collective-permute-start(bf16[256,256]{1,0:T(8,128)(2,1)S(1)} %maximum_select_fusion.5), channel_id=1, source_target_pairs={{0,2},{1,3},{2,0},{3,1},{4,6},{5,7},{6,4},{7,5},{8,10},{9,11},{10,... | collective-permute-start | bytes 393224 | tf_op jit(solution)/shard_map/ppermute | solution.py:27
Sparse Core Ops, SparseCore 0:
  31.7 37.1 reduce-scatter.3
  91.9 35.9 reduce-scatter.5
  150.8 35.8 reduce-scatter.7
